TPU v7x, 32 devices: a whole 2x2x4 slice. The times are simulated.
32 devices in a mesh: dp: 8 (over z, core), tensor: 4 (over y, x).
Axes of the slice: x: 2, y: 2, z: 4, core: 2. Of those that a mesh axis runs over, the one named last changes fastest.
Arguments:
- tokens: bfloat16 [32768, 1024], P(('dp', 'tensor')), may hold values from -6 to 6
- lengths: int32 [16], P('dp'), may hold values from 512 to 2048, as said below
- out_grad: bfloat16 [32768, 1024], P(('dp', 'tensor')), may hold values from -6 to 6
- ln1_gain: float32 [1024], replicated, may hold values from 0.5 to 1.5
- ln2_gain: float32 [1024], replicated, may hold values from 0.5 to 1.5
- onorm_gain: float32 [128], replicated, may hold values from 0.5 to 1.5
- a_log: float32 [8], replicated, may hold values from -6 to 0.5
- dt_bias: float32 [8], replicated, may hold values from -4 to 0
- w_query: bfloat16 [1024, 1024], P('dp', 'tensor'), may hold values from -0.1875 to 0.1875
- w_key: bfloat16 [1024, 2048], P('dp', 'tensor'), may hold values from -0.1875 to 0.1875
- w_value: bfloat16 [1024, 2048], P('dp', 'tensor'), may hold values from -0.1875 to 0.1875
- w_rates: bfloat16 [1024, 24], P('dp', 'tensor'), may hold values from -0.1875 to 0.1875
- w_outgate: bfloat16 [1024, 1024], P('dp', 'tensor'), may hold values from -0.1875 to 0.1875
- w_out: bfloat16 [1024, 1024], P('tensor', 'dp'), may hold values from -0.375 to 0.375
- w_gate: bfloat16 [1024, 2816], P('dp', 'tensor'), may hold values from -0.1875 to 0.1875
- w_up: bfloat16 [1024, 2816], P('dp', 'tensor'), may hold values from -0.1875 to 0.1875
- w_down: bfloat16 [2816, 1024], P('tensor', 'dp'), may hold values from -0.21875 to 0.21875
Outputs:
- block_out: bfloat16 [32768, 1024], P(('dp', 'tensor'))
- tokens_grad: bfloat16 [32768, 1024], P(('dp', 'tensor'))
- ln1_gain_grad: float32 [1024], replicated
- ln2_gain_grad: float32 [1024], replicated
- onorm_gain_grad: float32 [128], replicated
- a_log_grad: float32 [8], replicated
- dt_bias_grad: float32 [8], replicated
- w_query_grad: float32 [1024, 1024], P('dp', 'tensor')
- w_key_grad: float32 [1024, 2048], P('dp', 'tensor')
- w_value_grad: float32 [1024, 2048], P('dp', 'tensor')
- w_rates_grad: float32 [1024, 24], P('dp', 'tensor')
- w_outgate_grad: float32 [1024, 1024], P('dp', 'tensor')
- w_out_grad: float32 [1024, 1024], P('tensor', 'dp')
- w_gate_grad: float32 [1024, 2816], P('dp', 'tensor')
- w_up_grad: float32 [1024, 2816], P('dp', 'tensor')
- w_down_grad: float32 [2816, 1024], P('tensor', 'dp')
Inputs may be any that keep to these rules, and one draw needn't show every extreme that they name: `lengths`: valid positions of each sequence; the positions after them are padding; in every draw some sequence has all 2048 positions valid.
All inputs are finite; a program needn't handle non-finite values.
Results may differ from a plain program's by a relative error of at most 0.017.
Values may be sent and summed in bfloat16 or wider, within the bound.
No kernel may reach another device: no remote copies, remote signals or barrier semaphores. Data moves between devices by JAX's collectives and lax.ppermute only.
A program may use at most 448 MiB of HBM per device.

v0:
```python
from functools import partial
import jax
import jax.numpy as jnp
from jax import lax
from jax.sharding import PartitionSpec as P

HEAD = 128
NH = 2
CT = 64
LEN = 2048
HIGH = lax.Precision.HIGHEST
EPS = 1e-06


def project(left, right):
    return jnp.dot(left, right, preferred_element_type=jnp.float32)


def times_trans(left, right):
    return lax.dot_general(
        left, right, (((1,), (1,)), ((), ())), preferred_element_type=jnp.float32
    )


def trans_times(left, right):
    return lax.dot_general(
        left, right, (((0,), (0,)), ((), ())), preferred_element_type=jnp.float32
    )


def rms_parts(values):
    scale = lax.rsqrt(jnp.mean(values * values, axis=-1, keepdims=True) + EPS)
    return (values * scale, scale)


def rms_back(grad_out, values, scale, gain):
    gain_grad = jnp.sum(grad_out * values * scale, axis=0)
    scaled = grad_out * gain
    value_grad = scale * scaled - values * scale * scale * scale * jnp.mean(
        scaled * values, axis=-1, keepdims=True
    )
    return (value_grad, gain_grad)


def unit_rows(values):
    return values * lax.rsqrt(jnp.sum(values * values, axis=-1, keepdims=True) + EPS)


def stretch_mixer(query, keys, values, betas, decays):
    batch, length, heads, width = query.shape
    steps = keys.shape[3]
    vwidth = values.shape[-1]
    span = CT * steps
    nblock = length // CT

    def blocked(array):
        moved = array.reshape((batch, nblock, CT, heads) + array.shape[3:])
        return jnp.moveaxis(jnp.moveaxis(moved, 1, 0), 3, 2)

    queries = blocked(query)
    key_rows = blocked(keys).reshape(nblock, batch, heads, span, width)
    value_rows = blocked(values).reshape(nblock, batch, heads, span, vwidth)
    beta_rows = blocked(betas).reshape(nblock, batch, heads, span)
    log_decay = jnp.concatenate(
        [decays[..., None], jnp.zeros(decays.shape + (steps - 1,), jnp.float32)], axis=-1
    )
    cumul = jnp.cumsum(blocked(log_decay).reshape(nblock, batch, heads, span), axis=-1)
    index = jnp.arange(span)
    strict = index[:, None] > index[None, :]
    apart = cumul[..., :, None] - cumul[..., None, :]
    weights_strict = jnp.where(strict, jnp.exp(jnp.minimum(apart, 0.0)), 0.0)
    intersections = jnp.einsum("nbhid,nbhjd->nbhij", key_rows, key_rows, precision=HIGH)
    lower = (
        jnp.eye(span, dtype=jnp.float32) + weights_strict * intersections * beta_rows[..., None, :]
    )
    growth = jnp.exp(cumul)
    solved = jax.scipy.linalg.solve_triangular(
        lower,
        jnp.concatenate([value_rows, growth[..., None] * key_rows], axis=-1),
        lower=True,
        unit_diagonal=True,
    )
    new_values = solved[..., :vwidth]
    key_mix = solved[..., vwidth:]
    read_at = jnp.arange(CT) * steps + steps - 1
    read_cumul = cumul.reshape(nblock, batch, heads, CT, steps)[..., steps - 1]
    read_apart = read_cumul[..., :, None] - cumul[..., None, :]
    upto = read_at[:, None] >= index[None, :]
    read_weights = jnp.where(upto, jnp.exp(jnp.minimum(read_apart, 0.0)), 0.0)
    scores = (
        jnp.einsum("nbhid,nbhjd->nbhij", queries, key_rows, precision=HIGH)
        * read_weights
        * beta_rows[..., None, :]
    )
    query_decayed = jnp.exp(read_cumul)[..., None] * queries
    tail = cumul[..., span - 1]
    key_out = (jnp.exp(tail[..., None] - cumul) * beta_rows)[..., None] * key_rows

    def advance(carried, block_in):
        new_v, mix_k, score, query_d, key_o, tail_b = block_in
        delta = new_v - jnp.einsum("bhpk,bhkv->bhpv", mix_k, carried, precision=HIGH)
        output = jnp.einsum("bhck,bhkv->bhcv", query_d, carried, precision=HIGH) + jnp.einsum(
            "bhcp,bhpv->bhcv", score, delta, precision=HIGH
        )
        carried = jnp.exp(tail_b)[..., None, None] * carried + jnp.einsum(
            "bhpk,bhpv->bhkv", key_o, delta, precision=HIGH
        )
        return (carried, output)

    initial = jnp.zeros((batch, heads, width, vwidth), jnp.float32)
    last_state, outputs = lax.scan(
        advance, initial, (new_values, key_mix, scores, query_decayed, key_out, tail)
    )
    outputs = jnp.moveaxis(jnp.moveaxis(outputs, 2, 3), 0, 1)
    return outputs.reshape(batch, length, heads, vwidth)


def mixer(query_pre, key_pre, value_pre, rates_pre, outgate_pre, a_here, dt_here, gain, seq_count):
    rows = query_pre.shape[0]
    lead_dims = (seq_count, rows // seq_count)
    heads = a_here.shape[0]
    query = unit_rows(jax.nn.silu(query_pre).reshape(lead_dims + (heads, HEAD)))
    keys = unit_rows(jax.nn.silu(key_pre).reshape(lead_dims + (heads, NH, HEAD)))
    values = jax.nn.silu(value_pre).reshape(lead_dims + (heads, NH, HEAD))
    rates = rates_pre.reshape(lead_dims + (heads, NH + 1))
    betas = jax.nn.sigmoid(rates[..., :NH])
    decays = -jnp.exp(a_here) * jax.nn.softplus(rates[..., NH] + dt_here)
    mixed = stretch_mixer(query, keys, values, betas, decays)
    gate = jax.nn.silu(outgate_pre.reshape(lead_dims + (heads, HEAD)))
    normed = mixed * lax.rsqrt(jnp.mean(mixed * mixed, axis=-1, keepdims=True) + EPS) * gain * gate
    return normed.reshape(rows, heads * HEAD)


def per_device(
    tokens,
    lengths,
    out_grad,
    ln1_gain,
    ln2_gain,
    onorm_gain,
    a_log,
    dt_bias,
    w_query,
    w_key,
    w_value,
    w_rates,
    w_outgate,
    w_out,
    w_gate,
    w_up,
    w_down,
):
    tensor_count = lax.axis_size("tensor")
    tensor_pos = lax.axis_index("tensor")
    tok_dev = tokens.shape[0]
    seq_count = lengths.shape[0]
    heads_here = a_log.shape[0] // tensor_count
    positions = tensor_pos * tok_dev + jnp.arange(tok_dev)
    owners = positions // LEN
    limits = jnp.sum(
        jnp.where(owners[:, None] == jnp.arange(seq_count)[None, :], lengths[None, :], 0), axis=1
    )
    mask = (positions % LEN < limits).astype(jnp.float32)[:, None]
    full_query, full_key, full_value, full_rates, full_outgate, full_out = (
        lax.all_gather(w_query, "dp", axis=0, tiled=True),
        lax.all_gather(w_key, "dp", axis=0, tiled=True),
        lax.all_gather(w_value, "dp", axis=0, tiled=True),
        lax.all_gather(w_rates, "dp", axis=0, tiled=True),
        lax.all_gather(w_outgate, "dp", axis=0, tiled=True),
        lax.all_gather(w_out, "dp", axis=1, tiled=True),
    )
    resid_in = tokens.astype(jnp.float32)
    normed_one, scale_one = rms_parts(resid_in)
    first_all = lax.all_gather(
        (normed_one * ln1_gain).astype(jnp.bfloat16), "tensor", axis=0, tiled=True
    )
    query_pre = project(first_all, full_query)
    key_pre = project(first_all, full_key)
    value_pre = project(first_all, full_value)
    rates_pre = project(first_all, full_rates)
    outgate_pre = project(first_all, full_outgate)
    a_here = lax.dynamic_slice_in_dim(a_log, tensor_pos * heads_here, heads_here)
    dt_here = lax.dynamic_slice_in_dim(dt_bias, tensor_pos * heads_here, heads_here)
    mixed, mixer_back = jax.vjp(
        partial(mixer, seq_count=seq_count),
        query_pre,
        key_pre,
        value_pre,
        rates_pre,
        outgate_pre,
        a_here,
        dt_here,
        onorm_gain,
    )
    mixed_low = mixed.astype(jnp.bfloat16)
    attn_sum = lax.psum_scatter(
        project(mixed_low, full_out), "tensor", scatter_dimension=0, tiled=True
    )
    middle = resid_in + attn_sum
    full_gate, full_up, full_down = (
        lax.all_gather(w_gate, "dp", axis=0, tiled=True),
        lax.all_gather(w_up, "dp", axis=0, tiled=True),
        lax.all_gather(w_down, "dp", axis=1, tiled=True),
    )
    normed_two, scale_two = rms_parts(middle)
    second_all = lax.all_gather(
        (normed_two * ln2_gain).astype(jnp.bfloat16), "tensor", axis=0, tiled=True
    )
    gate_pre = project(second_all, full_gate)
    up_pre = project(second_all, full_up)
    gate_sig = jax.nn.sigmoid(gate_pre)
    gate_act = gate_pre * gate_sig
    hidden = (gate_act * up_pre).astype(jnp.bfloat16)
    mlp_sum = lax.psum_scatter(
        project(hidden, full_down).astype(jnp.bfloat16), "tensor", scatter_dimension=0, tiled=True
    ).astype(jnp.float32)
    block_out = ((middle + mlp_sum) * mask).astype(jnp.bfloat16)
    grad_top = out_grad.astype(jnp.float32) * mask
    grad_all = lax.all_gather(grad_top.astype(jnp.bfloat16), "tensor", axis=0, tiled=True)
    hidden_grad = times_trans(grad_all, full_down)
    down_grad = trans_times(hidden, grad_all)
    up_grad_pre = (hidden_grad * gate_act).astype(jnp.bfloat16)
    gate_grad_pre = (hidden_grad * up_pre * gate_sig * (1.0 + gate_pre * (1.0 - gate_sig))).astype(
        jnp.bfloat16
    )
    gate_grad = trans_times(second_all, gate_grad_pre)
    up_grad = trans_times(second_all, up_grad_pre)
    second_grad = lax.psum_scatter(
        times_trans(gate_grad_pre, full_gate) + times_trans(up_grad_pre, full_up),
        "tensor",
        scatter_dimension=0,
        tiled=True,
    )
    middle_back, ln2_grad = rms_back(second_grad, middle, scale_two, ln2_gain)
    middle_grad = grad_top + middle_back
    middle_low = middle_grad.astype(jnp.bfloat16)
    middle_all = lax.all_gather(middle_low, "tensor", axis=0, tiled=True)
    out_proj_grad = trans_times(mixed_low, middle_all)
    mixed_grad = times_trans(middle_all, full_out)
    pulled = mixer_back(mixed_grad)
    pre_grads = tuple((item.astype(jnp.bfloat16) for item in pulled[:5]))
    weights_full = (full_query, full_key, full_value, full_rates, full_outgate)
    proj_grads = tuple((trans_times(first_all, item) for item in pre_grads))
    first_part = times_trans(pre_grads[0], weights_full[0])
    for which in range(1, 5):
        first_part = first_part + times_trans(pre_grads[which], weights_full[which])
    first_grad = lax.psum_scatter(
        first_part.astype(jnp.bfloat16), "tensor", scatter_dimension=0, tiled=True
    ).astype(jnp.float32)
    input_back, ln1_grad = rms_back(first_grad, resid_in, scale_one, ln1_gain)
    tokens_grad = (middle_grad + input_back).astype(jnp.bfloat16)
    a_grad = lax.dynamic_update_slice_in_dim(
        jnp.zeros_like(a_log), pulled[5], tensor_pos * heads_here, 0
    )
    dt_grad = lax.dynamic_update_slice_in_dim(
        jnp.zeros_like(dt_bias), pulled[6], tensor_pos * heads_here, 0
    )
    small = lax.psum((ln1_grad, ln2_grad, pulled[7], a_grad, dt_grad), ("dp", "tensor"))
    summed = (
        lax.psum_scatter(
            proj_grads[0].astype(jnp.bfloat16), "dp", scatter_dimension=0, tiled=True
        ).astype(jnp.float32),
        lax.psum_scatter(
            proj_grads[1].astype(jnp.bfloat16), "dp", scatter_dimension=0, tiled=True
        ).astype(jnp.float32),
        lax.psum_scatter(
            proj_grads[2].astype(jnp.bfloat16), "dp", scatter_dimension=0, tiled=True
        ).astype(jnp.float32),
        lax.psum_scatter(
            proj_grads[3].astype(jnp.bfloat16), "dp", scatter_dimension=0, tiled=True
        ).astype(jnp.float32),
        lax.psum_scatter(
            proj_grads[4].astype(jnp.bfloat16), "dp", scatter_dimension=0, tiled=True
        ).astype(jnp.float32),
        lax.psum_scatter(
            out_proj_grad.astype(jnp.bfloat16), "dp", scatter_dimension=1, tiled=True
        ).astype(jnp.float32),
        lax.psum_scatter(
            gate_grad.astype(jnp.bfloat16), "dp", scatter_dimension=0, tiled=True
        ).astype(jnp.float32),
        lax.psum_scatter(
            up_grad.astype(jnp.bfloat16), "dp", scatter_dimension=0, tiled=True
        ).astype(jnp.float32),
        lax.psum_scatter(
            down_grad.astype(jnp.bfloat16), "dp", scatter_dimension=1, tiled=True
        ).astype(jnp.float32),
    )
    return (
        block_out,
        tokens_grad,
        small[0],
        small[1],
        small[2],
        small[3],
        small[4],
        summed[0],
        summed[1],
        summed[2],
        summed[3],
        summed[4],
        summed[5],
        summed[6],
        summed[7],
        summed[8],
    )


def solution(mesh):
    in_specs = (
        P(("dp", "tensor"), None),
        P("dp"),
        P(("dp", "tensor"), None),
        P(),
        P(),
        P(),
        P(),
        P(),
        P("dp", "tensor"),
        P("dp", "tensor"),
        P("dp", "tensor"),
        P("dp", "tensor"),
        P("dp", "tensor"),
        P("tensor", "dp"),
        P("dp", "tensor"),
        P("dp", "tensor"),
        P("tensor", "dp"),
    )
    out_specs = (
        P(("dp", "tensor"), None),
        P(("dp", "tensor"), None),
        P(),
        P(),
        P(),
        P(),
        P(),
        P("dp", "tensor"),
        P("dp", "tensor"),
        P("dp", "tensor"),
        P("dp", "tensor"),
        P("dp", "tensor"),
        P("tensor", "dp"),
        P("dp", "tensor"),
        P("dp", "tensor"),
        P("tensor", "dp"),
    )
    return jax.shard_map(
        per_device, mesh=mesh, in_specs=in_specs, out_specs=out_specs, check_vma=False
    )
```

profile of v0, /device:TPU:0, one launch (start us, length us, event | category | flops | bytes accessed | tf_op | source)
XLA Modules:
  0.0 3971.7 jit_solution(5733695194731297895)
XLA Ops:
  75.1 49.1 %all-gather.10.cloned.1.call-done = bf16[4096,1024]{1,0:T(8,128)(2,1)} async-done(((bf16[1024,1024]{1,0:T(8,128)(2,1)}), bf16[4096,1024]{1,0:T(8,128)(2,1)}) %all-gather.10.cloned.1.call-update) | async-done | bytes 8388624 | tf_op jit(solution)/shard_map/all_gather | solution.py:174
  265.2 21.4 fusion.218
  296.1 1259.2 %custom-call.10 = f32[32,2,2,1,128,128]{4,5,3,2,1,0:T(8,128)} custom-call(f32[32,2,2,1,128,128]{5,4,3,2,1,0:T(8,128)} %add_bitcast_fusion), custom_call_target="InvertDiagBlocksLowerTriangular" | custom-call | tf_op jit(solution)/shard_map/jvp(jit(_solve_triangular))/vmap(vmap(vmap()))/triangular_solve | solution.py:77
  1565.6 23.1 fusion.75
  1616.0 19.6 fusion.153
  1646.7 263.2 %while.48 = (s32[]{:T(128)}, f32[2,2,128,128]{3,2,1,0:T(8,128)S(1)}, f32[32,2,2,64,128]{4,3,2,1,0:T(8,128)}, f32[32,2,2,128,128]{4,3,2,1,0:T(8,128)}, f32[32,2,2...) while((s32[]{:T(128)}, ...), condition=%wide.region_5.6_spmd.clone, body=%wide.region_4.5_spmd.clone.sunk | while | flops 302481408 | bytes 4070101 | solution.py:111
  1951.8 153.5 %reduce-scatter.24.cloned.1.call-done = f32[1024,1024]{1,0:T(8,128)} async-done(((f32[4096,1024]{1,0:T(8,128)}), f32[1024,1024]{1,0:T(8,128)}) %reduce-scatter.24.cloned.1.call-update) | async-done | bytes 4194320 | tf_op jit(solution)/shard_map/reduce_scatter | solution.py:196
  2115.3 18.0 all-gather.18.cloned.1.call-done
  2133.3 88.6 %all-gather.16.cloned.1.call-done = bf16[4096,1024]{1,0:T(8,128)(2,1)} async-done(((bf16[1024,1024]{1,0:T(8,128)(2,1)}), bf16[4096,1024]{1,0:T(8,128)(2,1)}) %all-gather.16.cloned.1.call-update) | async-done | bytes 8388624 | tf_op jit(solution)/shard_map/all_gather | solution.py:206
  2277.0 88.8 %all-gather.24.cloned.1.call-done = bf16[4096,1024]{1,0:T(8,128)(2,1)} async-done(((bf16[1024,1024]{1,0:T(8,128)(2,1)}), bf16[4096,1024]{1,0:T(8,128)(2,1)}) %all-gather.24.cloned.1.call-update) | async-done | bytes 8388624 | tf_op jit(solution)/shard_map/all_gather | solution.py:219
  2365.8 22.4 multiply_convert_fusion
  2428.6 140.9 %reduce-scatter.28.cloned.1.call-done = f32[1024,1024]{1,0:T(8,128)} async-done(((f32[4096,1024]{1,0:T(8,128)}), f32[1024,1024]{1,0:T(8,128)}) %reduce-scatter.28.cloned.1.call-update) | async-done | bytes 4194320 | tf_op jit(solution)/shard_map/reduce_scatter | solution.py:228
  2574.6 84.4 %reduce-scatter.26.cloned.1.call-done = bf16[1024,1024]{1,0:T(8,128)(2,1)} async-done(((bf16[4096,1024]{1,0:T(8,128)(2,1)}), bf16[1024,1024]{1,0:T(8,128)(2,1)}) %reduce-scatter.26.cloned.1.call-update) | async-done | bytes 2097168 | tf_op jit(solution)/shard_map/reduce_scatter | solution.py:214
  2733.9 20.0 all-gather.26.cloned.1.call-done
  2804.5 588.0 %while.49 = (s32[]{:T(128)}, f32[2,2,128,128]{3,2,1,0:T(8,128)S(1)}, f32[32,2,2,128,128]{4,3,2,1,0:T(8,128)}, f32[32,2,2,128,128]{4,3,2,1,0:T(8,128)}, f32[32,2,...) while((s32[]{:T(128)}, ...), condition=%wide.region_16.17_spmd.clone, body=%wide.region_14.16_spmd.clone.sunk | while | flops 604766208 | bytes 6826808 | solution.py:111
  3392.5 23.8 fusion.80
  3416.3 21.4 fusion.79
  3437.7 22.1 fusion.93
  3476.9 19.7 fusion.105
  3496.6 17.3 multiply_reduce_fusion.1
  3558.1 24.3 add_add_fusion.1
  3799.6 25.5 add_convert_fusion
  3841.1 76.0 %reduce-scatter.30.cloned.1.call-done = bf16[1024,1024]{1,0:T(8,128)(2,1)} async-done(((bf16[4096,1024]{1,0:T(8,128)(2,1)}), bf16[1024,1024]{1,0:T(8,128)(2,1)}) %reduce-scatter.30.cloned.1.call-update) | async-done | bytes 2097168 | tf_op jit(solution)/shard_map/reduce_scatter | solution.py:247
  3920.3 39.6 all-reduce.7
  (1091 shorter events, 1694.5 us)
Async XLA Ops:
  7.2 67.9 %all-gather.12.cloned.1.call-start = ((), (), s32[]{:S(2)}) async-start(), calls=%async_computation.14 | async-start | bytes 1179648 | tf_op jit(solution)/shard_map/all_gather | solution.py:166
  8.0 116.2 %all-gather.10.cloned.1.call-start = ((), (), s32[]{:S(2)}) async-start(), calls=%async_computation.13 | async-start | bytes 10485760 | tf_op jit(solution)/shard_map/all_gather | solution.py:174
  13.6 217.7 %all-gather.14.cloned.1.call-start = ((), (), s32[]{:S(2)}) async-start(), calls=%async_computation.15 | async-start | bytes 1179648 | tf_op jit(solution)/shard_map/all_gather | solution.py:167
  14.4 2090.9 %reduce-scatter.24.cloned.1.call-start = ((), (), s32[]{:S(2)}) async-start(), calls=%async_computation.16 | async-start | bytes 20971520 | tf_op jit(solution)/shard_map/reduce_scatter | solution.py:196
  44.6 1571.4 %copy-start.83 = (pred[64,128]{1,0:T(8,128)(4,1)}, pred[64,128]{1,0:T(8,128)(4,1)S(1)}, u32[]{:S(2)}) copy-start(pred[64,128]{1,0:T(8,128)(4,1)S(1)} %iota_compare_fusion.4) | copy-start | bytes 24580
  201.8 1414.2 %copy-start.30 = (f32[32,2,2,128]{3,2,1,0:T(2,128)}, f32[32,2,2,128]{3,2,1,0:T(2,128)S(1)}, u32[]{:S(2)}) copy-start(f32[32,2,2,128]{3,2,1,0:T(2,128)S(1)} %copy.437) | copy-start | bytes 196612
  1951.2 182.1 %all-gather.18.cloned.1.call-start = ((), (), s32[]{:S(2)}) async-start(), calls=%async_computation.18 | async-start | bytes 1622016 | tf_op jit(solution)/shard_map/all_gather | solution.py:201
  1951.8 270.2 %all-gather.16.cloned.1.call-start = ((), (), s32[]{:S(2)}) async-start(), calls=%async_computation.17 | async-start | bytes 10485760 | tf_op jit(solution)/shard_map/all_gather | solution.py:206
  2111.8 138.3 %all-gather.20.cloned.1.call-start = ((), (), s32[]{:S(2)}) async-start(), calls=%async_computation.19 | async-start | bytes 1622016 | tf_op jit(solution)/shard_map/all_gather | solution.py:202
  2112.6 164.4 %all-gather.22.cloned.1.call-start = ((), (), s32[]{:S(2)}) async-start(), calls=%async_computation.20 | async-start | bytes 1622016 | tf_op jit(solution)/shard_map/all_gather | solution.py:203
  2113.3 252.4 %all-gather.24.cloned.1.call-start = ((), (), s32[]{:S(2)}) async-start(), calls=%async_computation.22 | async-start | bytes 10485760 | tf_op jit(solution)/shard_map/all_gather | solution.py:219
  2115.3 454.2 %reduce-scatter.28.cloned.1.call-start = ((), (), s32[]{:S(2)}) async-start(), calls=%async_computation.23 | async-start | bytes 20971520 | tf_op jit(solution)/shard_map/reduce_scatter | solution.py:228
  2415.5 243.5 %reduce-scatter.26.cloned.1.call-start = ((), (), s32[]{:S(2)}) async-start(), calls=%async_computation.21 | async-start | bytes 10485760 | tf_op jit(solution)/shard_map/reduce_scatter | solution.py:214
  2428.6 325.4 %all-gather.26.cloned.1.call-start = ((), (), s32[]{:S(2)}) async-start(), calls=%async_computation.24 | async-start | bytes 10485760 | tf_op jit(solution)/shard_map/all_gather | solution.py:237
  2666.2 1159.0 %reduce-scatter.44.cloned.1.call-start = ((), (), s32[]{:S(2)}) async-start(), calls=%async_computation.32 | async-start | bytes 1769472
  2678.1 1149.1 %reduce-scatter.46.cloned.1.call-start = ((), (), s32[]{:S(2)}) async-start(), calls=%async_computation.33 | async-start | bytes 1769472
  2690.0 1139.1 %reduce-scatter.48.cloned.1.call-start = ((), (), s32[]{:S(2)}) async-start(), calls=%async_computation.34 | async-start | bytes 1769472
  2733.7 1098.0 %reduce-scatter.40.cloned.1.call-start = ((), (), s32[]{:S(2)}) async-start(), calls=%async_computation.30 | async-start | bytes 294912
  3615.8 217.4 %reduce-scatter.42.cloned.1.call-start = ((), (), s32[]{:S(2)}) async-start(), calls=%async_computation.31 | async-start | bytes 589824
  3630.7 204.1 %reduce-scatter.32.cloned.1.call-start = ((), (), s32[]{:S(2)}) async-start(), calls=%async_computation.26 | async-start | bytes 589824 | tf_op jit(solution)/shard_map/reduce_scatter | solution.py:260
  3677.8 158.5 %reduce-scatter.38.cloned.1.call-start = ((), (), s32[]{:S(2)}) async-start(), calls=%async_computation.29 | async-start | bytes 589824 | tf_op jit(solution)/shard_map/reduce_scatter | solution.py:272
  3731.9 105.9 %reduce-scatter.34.cloned.1.call-start = ((), (), s32[]{:S(2)}) async-start(), calls=%async_computation.27 | async-start | bytes 1179648 | tf_op jit(solution)/shard_map/reduce_scatter | solution.py:263
  3755.7 83.7 %reduce-scatter.36.cloned.1.call-start = ((), (), s32[]{:S(2)}) async-start(), calls=%async_computation.28 | async-start | bytes 1179648 | tf_op jit(solution)/shard_map/reduce_scatter | solution.py:266
  3780.6 136.4 %reduce-scatter.30.cloned.1.call-start = ((), (), s32[]{:S(2)}) async-start(), calls=%async_computation.25 | async-start | bytes 10485760 | tf_op jit(solution)/shard_map/reduce_scatter | solution.py:247
  (124 other events, 8628.5 us)
Sparse Core Ops, SparseCore 0:
  9.6 24.8 all-gather.11
  36.9 87.2 all-gather.9
  125.8 22.0 all-gather.13
  1951.3 153.9 reduce-scatter.23
  2106.7 26.5 all-gather.17
  2135.6 86.3 all-gather.15
  2223.5 26.5 all-gather.19
  2251.7 25.2 all-gather.21
  2279.4 86.3 all-gather.23
  2415.6 153.8 reduce-scatter.27
  2572.6 86.4 reduce-scatter.25
  2666.3 87.5 all-gather.25
  2756.3 34.2 reduce-scatter.43
  2792.9 32.2 reduce-scatter.45
  2827.5 31.9 reduce-scatter.47
  3615.9 30.4 reduce-scatter.39
  3648.4 29.0 reduce-scatter.41
  3679.7 29.1 reduce-scatter.31
  3732.0 30.9 reduce-scatter.37
  3765.3 30.5 reduce-scatter.33
  3798.3 30.6 reduce-scatter.35
  3832.3 84.6 reduce-scatter.29
where the time goes:
time: 3990 us; the launch traced here: 3970 us
  other arithmetic  1550 us (39%)
  matrix products  1230 us (31%)
  waiting for transfers between devices  753 us (19%)
  local copies, waits for them, and re-layouts  322 us (8%)
  blocking collectives  99.2 us (2%)
    another operation x3, other arithmetic, stretch_mixer(): jax.scipy.linalg.solve_triangular(lower, jnp.concatenate([value_rows, gro...  1270 us
    dot_general x96, matrix products, advance(): jnp.einsum('bhcp,bhpv->bhcv', score, delta, precision=HIGH)  207 us
    dot_general x96, matrix products, advance(): jnp.einsum('bhpk,bhkv->bhpv', mix_k, carried, precision=HIGH)  192 us
    dot_general x96, matrix products, advance(): jnp.einsum('bhpk,bhpv->bhkv', key_o, delta, precision=HIGH)  168 us
    dot_general x96, matrix products, advance(): jnp.einsum('bhck,bhkv->bhcv', query_d, carried, precision=HIGH)  163 us
    reduce_scatter x1, waiting for transfers between devices, per_device(): lax.psum_scatter(project(mixed_low, full_out), 'tensor', scatter_dimensio...  153 us
    reduce_scatter x1, waiting for transfers between devices, per_device(): lax.psum_scatter(times_trans(gate_grad_pre, full_gate) + times_trans(up_g...  141 us
    dot_general x9, matrix products, times_trans(): lax.dot_general(left, right, (((1,), (1,)), ((), ())), preferred_element_...  124 us
  transfers between devices with their start and end apart: 22, of which 11 were waited for; matrix products, arithmetic and copies ran while one was open for 33% of the time, Pallas kernels for 0%

commit v1 on v0

--- a/solution.py
+++ b/solution.py
@@ -216,7 +216,25 @@
     ).astype(jnp.float32)
     block_out = ((middle + mlp_sum) * mask).astype(jnp.bfloat16)
     grad_top = out_grad.astype(jnp.float32) * mask
-    grad_all = lax.all_gather(grad_top.astype(jnp.bfloat16), "tensor", axis=0, tiled=True)
+    array_2 = grad_top.astype(jnp.bfloat16)
+    ways, here, step = (lax.axis_size("tensor"), lax.axis_index("tensor"), array_2.shape[0])
+    lengths_2 = [n * ways if d == 0 else n for d, n in enumerate(array_2.shape)]
+    grad_all = lax.dynamic_update_slice_in_dim(
+        jnp.zeros(lengths_2, array_2.dtype), array_2, here * step, axis=0
+    )
+    going_up = going_down = array_2
+    for far in range(1, ways // 2 + 1):
+        going_up = lax.ppermute(going_up, "tensor", [(d, (d + 1) % ways) for d in range(ways)])
+        grad_all = lax.dynamic_update_slice_in_dim(
+            grad_all, going_up, (here - far) % ways * step, axis=0
+        )
+        if 2 * far < ways:
+            going_down = lax.ppermute(
+                going_down, "tensor", [(d, (d - 1) % ways) for d in range(ways)]
+            )
+            grad_all = lax.dynamic_update_slice_in_dim(
+                grad_all, going_down, (here + far) % ways * step, axis=0
+            )
     hidden_grad = times_trans(grad_all, full_down)
     down_grad = trans_times(hidden, grad_all)
     up_grad_pre = (hidden_grad * gate_act).astype(jnp.bfloat16)

time: 3990 us -> 3980 us (level)
    ppermute x0 -> x3, waiting for transfers between devices: none -> 195 us  [the longest x2 117 us: per_device(): lax.ppermute(going_up, 'tensor', [(d, (d + 1) % ways) for d in range(ways)])]
    all_gather x1 -> x0, waiting for transfers between devices: 88.8 us -> none  [per_device(): lax.all_gather(grad_top.astype(jnp.bfloat16), 'tensor', axis=0, tiled=True)]
    all_gather x1, waiting for transfers between devices: 88.6 us -> 0.01 us  [per_device(): lax.all_gather((normed_two * ln2_gain).astype(jnp.bfloat16), 'tensor', ax...]
  transfers between devices with their start and end apart: 22 -> 24, of which waited for: 11 -> 9; matrix products, arithmetic and copies ran while one was open for 33% -> 33% of each run, Pallas kernels for 0% -> 0%
where the time goes in v1:
time: 3980 us; the launch traced here: 3960 us
  other arithmetic  1550 us (39%)
  matrix products  1230 us (31%)
  waiting for transfers between devices  721 us (18%)
  local copies, waits for them, and re-layouts  335 us (8%)
  blocking collectives  99.2 us (2%)
    another operation x3, other arithmetic, stretch_mixer(): jax.scipy.linalg.solve_triangular(lower, jnp.concatenate([value_rows, gro...  1270 us
    dot_general x96, matrix products, advance(): jnp.einsum('bhcp,bhpv->bhcv', score, delta, precision=HIGH)  208 us
    dot_general x96, matrix products, advance(): jnp.einsum('bhpk,bhkv->bhpv', mix_k, carried, precision=HIGH)  192 us
    dot_general x96, matrix products, advance(): jnp.einsum('bhpk,bhpv->bhkv', key_o, delta, precision=HIGH)  168 us
    dot_general x96, matrix products, advance(): jnp.einsum('bhck,bhkv->bhcv', query_d, carried, precision=HIGH)  163 us
    reduce_scatter x1, waiting for transfers between devices, per_device(): lax.psum_scatter(project(mixed_low, full_out), 'tensor', scatter_dimensio...  153 us
    reduce_scatter x1, waiting for transfers between devices, per_device(): lax.psum_scatter(times_trans(gate_grad_pre, full_gate) + times_trans(up_g...  141 us
    dot_general x9, matrix products, times_trans(): lax.dot_general(left, right, (((1,), (1,)), ((), ())), preferred_element_...  124 us
  transfers between devices with their start and end apart: 24, of which 9 were waited for; matrix products, arithmetic and copies ran while one was open for 33% of the time, Pallas kernels for 0%

profile of v1, /device:TPU:0, one launch (start us, length us, event | category | flops | bytes accessed | tf_op | source)
XLA Modules:
  0.0 3959.9 jit_solution(15148040263612115241)
XLA Ops:
  75.1 49.1 %all-gather.9.cloned.1.call-done = bf16[4096,1024]{1,0:T(8,128)(2,1)} async-done(((bf16[1024,1024]{1,0:T(8,128)(2,1)}), bf16[4096,1024]{1,0:T(8,128)(2,1)}) %all-gather.9.cloned.1.call-update) | async-done | bytes 8388624 | tf_op jit(solution)/shard_map/all_gather | solution.py:174
  265.3 21.4 fusion.219
  296.4 1259.2 %custom-call.10 = f32[32,2,2,1,128,128]{4,5,3,2,1,0:T(8,128)} custom-call(f32[32,2,2,1,128,128]{5,4,3,2,1,0:T(8,128)} %add_bitcast_fusion), custom_call_target="InvertDiagBlocksLowerTriangular" | custom-call | tf_op jit(solution)/shard_map/jvp(jit(_solve_triangular))/vmap(vmap(vmap()))/triangular_solve | solution.py:77
  1565.9 23.1 fusion.75
  1616.6 19.6 fusion.153
  1647.3 263.2 %while.48 = (s32[]{:T(128)}, f32[2,2,128,128]{3,2,1,0:T(8,128)S(1)}, f32[32,2,2,64,128]{4,3,2,1,0:T(8,128)}, f32[32,2,2,128,128]{4,3,2,1,0:T(8,128)}, f32[32,2,2...) while((s32[]{:T(128)}, ...), condition=%wide.region_5.6_spmd.clone, body=%wide.region_4.5_spmd.clone.sunk | while | flops 302481408 | bytes 4070101 | solution.py:111
  1952.4 153.5 %reduce-scatter.24.cloned.1.call-done = f32[1024,1024]{1,0:T(8,128)} async-done(((f32[4096,1024]{1,0:T(8,128)}), f32[1024,1024]{1,0:T(8,128)}) %reduce-scatter.24.cloned.1.call-update) | async-done | bytes 4194320 | tf_op jit(solution)/shard_map/reduce_scatter | solution.py:196
  2122.5 68.2 %collective-permute-done = bf16[1024,1024]{1,0:T(8,128)(2,1)} collective-permute-done((bf16[1024,1024]{1,0:T(8,128)(2,1)}, bf16[1024,1024]{1,0:T(8,128)(2,1)}, u32[]{:S(2)}, u32[]{:S(2)}) %collective-permute-start) | collective-permute-done | bytes 2097184 | tf_op jit(solution)/shard_map/ppermute | solution.py:227
  2195.4 78.1 %collective-permute-done.1 = bf16[1024,1024]{1,0:T(8,128)(2,1)} collective-permute-done((bf16[1024,1024]{1,0:T(8,128)(2,1)}, bf16[1024,1024]{1,0:T(8,128)(2,1)}, u32[]{:S(2)}, u32[]{:S(2)}) %collective-permute-start.1) | collective-permute-done | bytes 2097184 | tf_op jit(solution)/shard_map/ppermute | solution.py:232
  2276.6 48.7 %collective-permute-done.2 = bf16[1024,1024]{1,0:T(8,128)(2,1)} collective-permute-done((bf16[1024,1024]{1,0:T(8,128)(2,1)}, bf16[1024,1024]{1,0:T(8,128)(2,1)}, u32[]{:S(2)}, u32[]{:S(2)}) %collective-permute-start.2) | collective-permute-done | bytes 2097184 | tf_op jit(solution)/shard_map/ppermute | solution.py:227
  2353.8 22.6 multiply_convert_fusion
  2416.7 140.8 %reduce-scatter.28.cloned.1.call-done = f32[1024,1024]{1,0:T(8,128)} async-done(((f32[4096,1024]{1,0:T(8,128)}), f32[1024,1024]{1,0:T(8,128)}) %reduce-scatter.28.cloned.1.call-update) | async-done | bytes 4194320 | tf_op jit(solution)/shard_map/reduce_scatter | solution.py:246
  2562.7 84.2 %reduce-scatter.26.cloned.1.call-done = bf16[1024,1024]{1,0:T(8,128)(2,1)} async-done(((bf16[4096,1024]{1,0:T(8,128)(2,1)}), bf16[1024,1024]{1,0:T(8,128)(2,1)}) %reduce-scatter.26.cloned.1.call-update) | async-done | bytes 2097168 | tf_op jit(solution)/shard_map/reduce_scatter | solution.py:214
  2721.8 20.0 all-gather.23.cloned.1.call-done
  2792.4 588.6 %while.49 = (s32[]{:T(128)}, f32[2,2,128,128]{3,2,1,0:T(8,128)S(1)}, f32[32,2,2,128,128]{4,3,2,1,0:T(8,128)}, f32[32,2,2,128,128]{4,3,2,1,0:T(8,128)}, f32[32,2,...) while((s32[]{:T(128)}, ...), condition=%wide.region_16.17_spmd.clone, body=%wide.region_14.16_spmd.clone.sunk | while | flops 604766208 | bytes 6826808 | solution.py:111
  3381.0 23.8 fusion.80
  3404.8 21.4 fusion.79
  3426.2 22.1 fusion.93
  3465.4 19.7 fusion.105
  3485.1 17.3 multiply_reduce_fusion.1
  3546.6 24.3 add_add_fusion.1
  3788.0 25.5 add_convert_fusion
  3829.4 75.8 %reduce-scatter.30.cloned.1.call-done = bf16[1024,1024]{1,0:T(8,128)(2,1)} async-done(((bf16[4096,1024]{1,0:T(8,128)(2,1)}), bf16[1024,1024]{1,0:T(8,128)(2,1)}) %reduce-scatter.30.cloned.1.call-update) | async-done | bytes 2097168 | tf_op jit(solution)/shard_map/reduce_scatter | solution.py:265
  3908.5 39.6 all-reduce.7
  (1098 shorter events, 1683.7 us)
Async XLA Ops:
  7.2 67.9 %all-gather.11.cloned.1.call-start = ((), (), s32[]{:S(2)}) async-start(), calls=%async_computation.14 | async-start | bytes 1179648 | tf_op jit(solution)/shard_map/all_gather | solution.py:166
  8.0 116.2 %all-gather.9.cloned.1.call-start = ((), (), s32[]{:S(2)}) async-start(), calls=%async_computation.13 | async-start | bytes 10485760 | tf_op jit(solution)/shard_map/all_gather | solution.py:174
  13.6 217.8 %all-gather.13.cloned.1.call-start = ((), (), s32[]{:S(2)}) async-start(), calls=%async_computation.15 | async-start | bytes 1179648 | tf_op jit(solution)/shard_map/all_gather | solution.py:167
  14.4 2091.5 %reduce-scatter.24.cloned.1.call-start = ((), (), s32[]{:S(2)}) async-start(), calls=%async_computation.16 | async-start | bytes 20971520 | tf_op jit(solution)/shard_map/reduce_scatter | solution.py:196
  1951.7 376.8 %all-gather.17.cloned.1.call-start = ((), (), s32[]{:S(2)}) async-start(), calls=%async_computation.18 | async-start | bytes 1622016 | tf_op jit(solution)/shard_map/all_gather | solution.py:201
  1952.3 376.2 %all-gather.15.cloned.1.call-start = ((), (), s32[]{:S(2)}) async-start(), calls=%async_computation.17 | async-start | bytes 10485760 | tf_op jit(solution)/shard_map/all_gather | solution.py:206
  2112.5 228.7 %all-gather.19.cloned.1.call-start = ((), (), s32[]{:S(2)}) async-start(), calls=%async_computation.19 | async-start | bytes 1622016 | tf_op jit(solution)/shard_map/all_gather | solution.py:202
  2119.5 71.2 %collective-permute-start = (bf16[1024,1024]{1,0:T(8,128)(2,1)}, bf16[1024,1024]{1,0:T(8,128)(2,1)}, u32[]{:S(2)}, u32[]{:S(2)}) collective-permute-start(bf16[1024,1024]{1,0:T(8,128)(2,1)} %get-tuple-element.852), channel_id=1, source_target_pairs={{0,1},{1,2},{2,3},{3,0},{4,5},{5,6},{6,7},{7,4},{8,9},{9,10},{10,1... | collective-permute-start | bytes 6291464 | tf_op jit(solution)/shard_map/ppermute | solution.py:227
  2120.9 232.9 %all-gather.21.cloned.1.call-start = ((), (), s32[]{:S(2)}) async-start(), calls=%async_computation.20 | async-start | bytes 1622016 | tf_op jit(solution)/shard_map/all_gather | solution.py:203
  2120.9 152.6 %collective-permute-start.1 = (bf16[1024,1024]{1,0:T(8,128)(2,1)}, bf16[1024,1024]{1,0:T(8,128)(2,1)}, u32[]{:S(2)}, u32[]{:S(2)}) collective-permute-start(bf16[1024,1024]{1,0:T(8,128)(2,1)} %get-tuple-element.852), channel_id=1, source_target_pairs={{0,3},{1,0},{2,1},{3,2},{4,7},{5,4},{6,5},{7,6},{8,11},{9,8},{10,9... | collective-permute-start | bytes 6291464 | tf_op jit(solution)/shard_map/ppermute | solution.py:232
  2190.7 134.6 %collective-permute-start.2 = (bf16[1024,1024]{1,0:T(8,128)(2,1)}, bf16[1024,1024]{1,0:T(8,128)(2,1)}, u32[]{:S(2)}, u32[]{:S(2)}) collective-permute-start(bf16[1024,1024]{1,0:T(8,128)(2,1)} %collective-permute-done), channel_id=1, source_target_pairs={{0,1},{1,2},{2,3},{3,0},{4,5},{5,6},{6,7},{7,4},{8,9},{9,10},{10,1... | collective-permute-start | bytes 6291464 | tf_op jit(solution)/shard_map/ppermute | solution.py:227
  2192.2 365.4 %reduce-scatter.28.cloned.1.call-start = ((), (), s32[]{:S(2)}) async-start(), calls=%async_computation.22 | async-start | bytes 20971520 | tf_op jit(solution)/shard_map/reduce_scatter | solution.py:246
  2403.6 243.2 %reduce-scatter.26.cloned.1.call-start = ((), (), s32[]{:S(2)}) async-start(), calls=%async_computation.21 | async-start | bytes 10485760 | tf_op jit(solution)/shard_map/reduce_scatter | solution.py:214
  2416.7 325.1 %all-gather.23.cloned.1.call-start = ((), (), s32[]{:S(2)}) async-start(), calls=%async_computation.23 | async-start | bytes 10485760 | tf_op jit(solution)/shard_map/all_gather | solution.py:255
  2654.1 1159.5 %reduce-scatter.44.cloned.1.call-start = ((), (), s32[]{:S(2)}) async-start(), calls=%async_computation.31 | async-start | bytes 1769472
  2665.9 1149.6 %reduce-scatter.46.cloned.1.call-start = ((), (), s32[]{:S(2)}) async-start(), calls=%async_computation.32 | async-start | bytes 1769472
  2677.9 1139.6 %reduce-scatter.48.cloned.1.call-start = ((), (), s32[]{:S(2)}) async-start(), calls=%async_computation.33 | async-start | bytes 1769472
  2721.6 1098.5 %reduce-scatter.40.cloned.1.call-start = ((), (), s32[]{:S(2)}) async-start(), calls=%async_computation.29 | async-start | bytes 294912
  3604.2 217.3 %reduce-scatter.42.cloned.1.call-start = ((), (), s32[]{:S(2)}) async-start(), calls=%async_computation.30 | async-start | bytes 589824
  3619.1 204.0 %reduce-scatter.32.cloned.1.call-start = ((), (), s32[]{:S(2)}) async-start(), calls=%async_computation.25 | async-start | bytes 589824 | tf_op jit(solution)/shard_map/reduce_scatter | solution.py:278
  3666.2 158.4 %reduce-scatter.38.cloned.1.call-start = ((), (), s32[]{:S(2)}) async-start(), calls=%async_computation.28 | async-start | bytes 589824 | tf_op jit(solution)/shard_map/reduce_scatter | solution.py:290
  3720.3 105.9 %reduce-scatter.34.cloned.1.call-start = ((), (), s32[]{:S(2)}) async-start(), calls=%async_computation.26 | async-start | bytes 1179648 | tf_op jit(solution)/shard_map/reduce_scatter | solution.py:281
  3744.1 83.7 %reduce-scatter.36.cloned.1.call-start = ((), (), s32[]{:S(2)}) async-start(), calls=%async_computation.27 | async-start | bytes 1179648 | tf_op jit(solution)/shard_map/reduce_scatter | solution.py:284
  3769.0 136.2 %reduce-scatter.30.cloned.1.call-start = ((), (), s32[]{:S(2)}) async-start(), calls=%async_computation.24 | async-start | bytes 10485760 | tf_op jit(solution)/shard_map/reduce_scatter | solution.py:265
  (126 other events, 11514.0 us)
Sparse Core Ops, SparseCore 0:
  9.6 24.8 all-gather.10
  36.9 87.2 all-gather.8
  125.8 22.0 all-gather.12
  1951.8 153.9 reduce-scatter.23
  2107.3 26.5 all-gather.16
  2136.1 153.4 all-gather.14
  2291.3 26.5 all-gather.18
  2319.4 25.2 all-gather.20
  2403.8 153.7 reduce-scatter.27
  2560.5 86.3 reduce-scatter.25
  2654.2 87.6 all-gather.22
  2744.1 34.2 reduce-scatter.43
  2780.8 32.3 reduce-scatter.45
  2815.5 32.1 reduce-scatter.47
  3604.3 30.2 reduce-scatter.39
  3636.8 29.1 reduce-scatter.41
  3668.2 29.0 reduce-scatter.31
  3720.4 30.9 reduce-scatter.37
  3753.7 30.5 reduce-scatter.33
  3786.5 30.5 reduce-scatter.35
  3820.4 84.7 reduce-scatter.29
